TPU v7x, 512 devices: a whole 4x8x8 slice. The times are simulated.
512 devices in a mesh: cuts: 4 (over y_hi, core), mode: 128 (over x, y_lo, z).
Axes of the slice: x: 4, y: 8 (y_hi: 2, y_lo: 4; y = y_hi * 4 + y_lo), z: 8, core: 2. Of those that a mesh axis runs over, the one named last changes fastest.
Arguments:
- stem: bfloat16 [4, 2, 1024, 16384], P('cuts', None, None, 'mode'), may hold values from -6 to 6
- branches: bfloat16 [3, 2, 1024, 1024], P(None, None, None, 'mode'), may hold values from -0.125 to 0.125
- order: int32 [3], replicated, may hold values from 0 to 2, each once
- swap_order: int32 [3, 1024], replicated, may hold values from 0 to 1023, each once within a row
- row_bits: int32 [2048], replicated, may hold values from 0 to 1023
- column_bits: int32 [2048], replicated, may hold values from 0 to 16383
Outputs:
- stem_out: bfloat16 [4, 2, 1024, 16384], P('cuts', None, None, 'mode')
- amplitudes: float32 [2, 2048], P(None, ('cuts', 'mode'))
All inputs are finite; a program needn't handle non-finite values.
Results may differ from a plain program's by a relative error of at most 0.009.
Values may be sent and summed in bfloat16 or wider, within the bound.
A program may use at most 128 MiB of HBM per device.

v0:
```python
import jax
import jax.numpy as jnp
from jax import lax
from jax.sharding import Mesh
from jax.sharding import PartitionSpec as P

MODE = ("mode_0", "mode_1", "mode_2")
CUTS_MODE = ("cuts_0", "cuts_1", "mode_0", "mode_1", "mode_2")
CUTS = ("cuts_0", "cuts_1")


def cut_rows(length, count):
    unit = 8 if length >= 8 * count else 1
    return [length // unit * k // count * unit for k in range(1, count)]


def gather_in_order(shard, axes, turns):
    blocks = shard[None]
    for k in turns:
        blocks = lax.all_gather(blocks, axes[k], axis=0, tiled=True)
    held = [lax.axis_size(axes[k]) for k in reversed(turns)]
    blocks = blocks.reshape(*held, *shard.shape)
    turned = sorted(range(len(turns)), key=lambda place: turns[len(turns) - 1 - place])
    return blocks.transpose(*turned, *range(len(turns), blocks.ndim)).reshape(-1, *shard.shape)


def joined_along(blocks, dim):
    blocks = jnp.moveaxis(blocks, 0, dim)
    dims = blocks.shape
    return blocks.reshape(*dims[:dim], dims[dim] * dims[dim + 1], *dims[dim + 2 :])


def gather_at_once(shard, axes, dim):
    cut = max(range(max(1, shard.ndim - 1)), key=lambda d: shard.shape[d])
    count, finished = (len(axes), [])
    for initial, slab in enumerate(jnp.split(shard, cut_rows(shard.shape[cut], count), axis=cut)):
        if slab.size:
            turns = [(initial - k) % count for k in range(count)]
            finished.append(gather_in_order(slab, axes, turns))
    return joined_along(jnp.concatenate(finished, axis=cut + 1), dim)


def over_axes(shard, axes):
    for axis in axes:
        shard = lax.psum(shard, axis)
    return shard


def absorb(matrix, part):
    numbers = (((0,), (0,)), ((), ()))

    def product(left, right):
        return lax.dot_general(left, right, numbers, preferred_element_type=jnp.float32)

    real = product(matrix[0], part[0]) - product(matrix[1], part[1])
    imag = product(matrix[0], part[1]) + product(matrix[1], part[0])
    return jnp.stack([real, imag], axis=0)


def body(stem, branches, order, swap_order, row_bits, column_bits):
    local = stem[0]
    groups = lax.axis_size(MODE)
    width = local.shape[1]
    rows = local.shape[2]
    everything = gather_at_once(branches, MODE, 3)
    for step in range(swap_order.shape[0]):
        moved = jnp.take(local, swap_order[step], axis=1)
        view = moved.reshape(2, groups, width // groups, rows)
        swapped = lax.all_to_all(view, MODE, split_axis=1, concat_axis=1, tiled=True)
        current = swapped.reshape(2, width, rows)
        pick = order[step]
        matrix = lax.dynamic_index_in_dim(everything, pick, 0, keepdims=False)
        local = absorb(matrix, current).astype(jnp.bfloat16)
    offset = lax.axis_index(MODE) * rows
    column_local = column_bits - offset
    inside = jnp.logical_and(column_local >= 0, column_local < rows)
    flat_index = row_bits * rows + jnp.clip(column_local, 0, rows - 1)
    flat = local.reshape(2, width * rows)
    values = jnp.take(flat, flat_index, axis=1).astype(jnp.float32)
    values = jnp.where(inside[None, :], values, jnp.zeros_like(values))
    total_amps = over_axes(values, CUTS_MODE)
    share = values.shape[1] // lax.axis_size(CUTS_MODE)
    amplitudes = lax.dynamic_slice_in_dim(total_amps, lax.axis_index(CUTS_MODE) * share, share, 1)
    return (local[None], amplitudes)


def solution(mesh):
    finer = Mesh(
        mesh.devices.reshape(2, 2, 4, 4, 8), ("cuts_0", "cuts_1", "mode_0", "mode_1", "mode_2")
    )
    placed = (P(CUTS, None, None, MODE), P(None, None, None, MODE), P(), P(), P(), P())
    return jax.shard_map(
        body,
        mesh=finer,
        in_specs=placed,
        out_specs=(P(CUTS, None, None, MODE), P(None, CUTS_MODE)),
        check_vma=False,
    )
```

profile of v0, /device:TPU:6, one launch (start us, length us, event | category | flops | bytes accessed | tf_op | source)
XLA Modules:
  0.0 672.4 jit_solution(10324625984427429543)
XLA Ops:
  7.2 0.9 fusion.45
  8.1 33.4 %all-gather.2 = bf16[24,2,344,8]{2,3,1,0:T(8,128)(2,1)} all-gather(bf16[3,2,344,8]{2,3,1,0:T(8,128)(2,1)S(1)} %get-tuple-element.14), channel_id=4, replica_groups=mesh['cuts_0'=2,'cuts_1'=2,'mode_0'=4,'mode_1'=4,'mode_2'=8] {'mode_2'}, dimensions={0}, use_global_device_ids=true | all-gather | bytes 297216 | tf_op jit(solution)/shard_map/all_gather | solution.py:20
  42.4 12.0 %all-gather = bf16[12,2,336,8]{2,3,1,0:T(8,128)(2,1)S(1)} all-gather(bf16[3,2,336,8]{2,3,1,0:T(8,128)(2,1)S(1)} %split.9), channel_id=2, replica_groups=mesh['cuts_0'=2,'cuts_1'=2,'mode_0'=4,'mode_1'=4,'mode_2'=8] {'mode_0'}, dimensions={0}, use_global_device_ids=true | all-gather | bytes 161280 | tf_op jit(solution)/shard_map/all_gather | solution.py:20
  54.4 29.2 %all_gather.28 = bf16[32,3,2,336,8]{3,4,2,1,0:T(8,128)(2,1)} all-gather(bf16[4,3,2,336,8]{3,4,2,1,0:T(8,128)(2,1)S(1)} %bitcast.161), channel_id=1, replica_groups=mesh['cuts_0'=2,'cuts_1'=2,'mode_0'=4,'mode_1'=4,'mode_2'=8] {'mode_2'}, dimensions={0}, use_global_device_ids=true | all-gather | bytes 1161216 | tf_op jit(solution)/shard_map/all_gather | solution.py:20
  83.6 13.6 %all-gather.1 = bf16[12,2,344,8]{2,3,1,0:T(8,128)(2,1)S(1)} all-gather(bf16[3,2,344,8]{2,3,1,0:T(8,128)(2,1)S(1)} %get-tuple-element.13), channel_id=3, replica_groups=mesh['cuts_0'=2,'cuts_1'=2,'mode_0'=4,'mode_1'=4,'mode_2'=8] {'mode_1'}, dimensions={0}, use_global_device_ids=true | all-gather | bytes 165120 | tf_op jit(solution)/shard_map/all_gather | solution.py:20
  97.3 13.6 %all_gather.31 = bf16[16,3,2,344,8]{3,4,2,1,0:T(8,128)(2,1)} all-gather(bf16[4,3,2,344,8]{3,4,2,1,0:T(8,128)(2,1)S(1)} %bitcast.162), channel_id=1, replica_groups=mesh['cuts_0'=2,'cuts_1'=2,'mode_0'=4,'mode_1'=4,'mode_2'=8] {'mode_0'}, dimensions={0}, use_global_device_ids=true | all-gather | bytes 660480 | tf_op jit(solution)/shard_map/all_gather | solution.py:20
  111.5 1.6 copy.70
  114.0 3.7 gather_fusion.1
  117.7 3.7 broadcast_select_fusion.2
  121.4 0.9 copy.45
  122.3 10.9 %all-to-all-start = ((bf16[2,128,8,128]{3,2,0,1:T(8,128)(2,1)}), bf16[2,128,8,128]{3,2,0,1:T(8,128)(2,1)S(1)}, u32[]{:S(2)}, u32[]{:S(2)}) async-start(bf16[2,128,8,128]{3,2,0,1:T(8,128)(2,1)} %copy.45), calls=%async_computation | async-start | bytes 1048576 | tf_op jit(solution)/shard_map/all_to_all | solution.py:69
  133.2 1.4 fusion.47
  136.6 48.5 %all-gather.8.cloned.1.call-done = bf16[128,3,2,336,8]{3,4,2,1,0:T(8,128)(2,1)} async-done(((bf16[32,3,2,336,8]{3,4,2,1,0:T(8,128)(2,1)}), bf16[128,3,2,336,8]{3,4,2,1,0:T(8,128)(2,1)}) %all-gather.8.cloned.1.call-update) | async-done | bytes 4128784 | tf_op jit(solution)/shard_map/all_gather | solution.py:20
  185.1 5.2 copy.41
  190.3 61.7 %all-gather.10.cloned.1.call-done = bf16[128,3,2,344,8]{3,4,2,1,0:T(8,128)(2,1)} async-done(((bf16[16,3,2,344,8]{3,4,2,1,0:T(8,128)(2,1)}), bf16[128,3,2,344,8]{3,4,2,1,0:T(8,128)(2,1)}) %all-gather.10.cloned.1.call-update) | async-done | bytes 4227088 | tf_op jit(solution)/shard_map/all_gather | solution.py:20
  252.0 5.2 copy.42
  257.2 51.1 %all-gather.14.cloned.1.call-done = bf16[128,3,2,344,8]{3,4,2,1,0:T(8,128)(2,1)} async-done(((bf16[32,3,2,344,8]{3,4,2,1,0:T(8,128)(2,1)}), bf16[128,3,2,344,8]{3,4,2,1,0:T(8,128)(2,1)}) %all-gather.14.cloned.1.call-update) | async-done | bytes 4227088 | tf_op jit(solution)/shard_map/all_gather | solution.py:20
  308.3 13.7 %copy_bitcast_fusion = bf16[3,2,1024,1024]{2,3,1,0:T(8,128)(2,1)} fusion(bf16[128,3,2,344,8]{3,4,2,1,0:T(8,128)(2,1)} %all-gather.14.cloned.1.call-done, bf16[128,3,2,344,8]{3,4,2,1,0:T(8,128)(2,1)} %bitcast.153, bf16[128,3,2,336,8]{3,4,2,1,0:T(8,128)(2,1)} %bitcast.152), kind=kLoop, calls=%fused_computation.5 | loop fusion | flops 37748736 | bytes 25165824 | tf_op jit(solution)/shard_map/reshape | solution.py:30
  322.0 2.3 fusion.5
  324.3 2.3 fusion.4
  326.6 2.3 fusion.28
  328.9 2.3 fusion.29
  331.9 3.7 gather_fusion.2
  335.6 3.7 broadcast_select_fusion.1
  339.3 0.9 copy.49
  340.2 15.8 %all-to-all-start.1 = ((bf16[2,128,8,128]{3,2,0,1:T(8,128)(2,1)}), bf16[2,128,8,128]{3,2,0,1:T(8,128)(2,1)S(1)}, u32[]{:S(2)}, u32[]{:S(2)}) async-start(bf16[2,128,8,128]{3,2,0,1:T(8,128)(2,1)} %copy.49), calls=%async_computation.1 | async-start | bytes 1048576 | tf_op jit(solution)/shard_map/all_to_all | solution.py:69
  358.1 14.8 %all-to-all-done.1 = bf16[2,128,8,128]{3,2,0,1:T(8,128)(2,1)S(1)} async-done(((bf16[2,128,8,128]{3,2,0,1:T(8,128)(2,1)}), bf16[2,128,8,128]{3,2,0,1:T(8,128)(2,1)S(1)}, u32[]{:S(2)}, u32[]{:S(2)}) %all-to-all-start.1) | async-done | bytes 524320 | tf_op jit(solution)/shard_map/all_to_all | solution.py:69
  372.9 2.3 fusion.3
  375.2 2.3 fusion.2
  377.5 2.3 fusion.26
  379.8 2.3 fusion.27
  382.7 3.7 gather_fusion.3
  386.4 3.7 broadcast_select_fusion
  390.2 0.9 copy.53
  391.0 9.1 %all-to-all-start.2 = ((bf16[2,128,8,128]{3,2,0,1:T(8,128)(2,1)}), bf16[2,128,8,128]{3,2,0,1:T(8,128)(2,1)S(1)}, u32[]{:S(2)}, u32[]{:S(2)}) async-start(bf16[2,128,8,128]{3,2,0,1:T(8,128)(2,1)} %copy.53), calls=%async_computation.2 | async-start | bytes 1048576 | tf_op jit(solution)/shard_map/all_to_all | solution.py:69
  402.1 14.7 %all-to-all-done.2 = bf16[2,128,8,128]{3,2,0,1:T(8,128)(2,1)S(1)} async-done(((bf16[2,128,8,128]{3,2,0,1:T(8,128)(2,1)}), bf16[2,128,8,128]{3,2,0,1:T(8,128)(2,1)S(1)}, u32[]{:S(2)}, u32[]{:S(2)}) %all-to-all-start.2) | async-done | bytes 524320 | tf_op jit(solution)/shard_map/all_to_all | solution.py:69
  416.8 2.3 fusion.1
  419.1 2.3 fusion
  421.4 2.3 fusion.24
  423.7 2.3 fusion.25
  427.7 1.2 pad_maximum_fusion.3
  428.9 20.3 %copy.56 = bf16[2,131072]{0,1:T(8,128)(2,1)} copy(bf16[2,131072]{1,0:T(2,128)(2,1)S(1)} %pad_maximum_fusion.3) | data formatting | bytes 1048576 | tf_op jit(solution)/shard_map/stack | solution.py:57
  449.1 21.5 %gather_fusion = bf16[2048,2]{1,0:T(8,128)(2,1)S(1)} fusion(bf16[2,131072]{0,1:T(8,128)(2,1)} %copy.56, s32[2048]{0:T(1024)S(1)} %broadcast_clamp_fusion), kind=kCustom, calls=%fused_computation.3 | custom fusion | bytes 24576 | tf_op jit(solution)/shard_map/jit(_take)/gather | solution.py:79
  471.4 42.2 %psum.35 = f32[2,2048]{0,1:T(8,128)S(1)} all-reduce(f32[2,2048]{0,1:T(8,128)S(1)} %select_bitcast_fusion), channel_id=1, replica_groups=mesh['cuts_0'=2,'cuts_1'=2,'mode_0'=4,'mode_1'=4,'mode_2'=8] {'cuts_0'}, use_global_device_ids=true, to_apply=%region_0.0 | all-reduce | flops 4096 | bytes 32768 | tf_op jit(solution)/shard_map/psum | solution.py:45
  513.6 5.7 psum.36
  519.2 31.3 %psum.37 = f32[2,2048]{0,1:T(8,128)S(1)} all-reduce(f32[2,2048]{0,1:T(8,128)S(1)} %psum.36), channel_id=1, replica_groups=mesh['cuts_0'=2,'cuts_1'=2,'mode_0'=4,'mode_1'=4,'mode_2'=8] {'mode_0'}, use_global_device_ids=true, to_apply=%region_2.4 | all-reduce | flops 4096 | bytes 32768 | tf_op jit(solution)/shard_map/psum | solution.py:45
  550.5 56.0 %psum.38 = f32[2,2048]{0,1:T(8,128)S(1)} all-reduce(f32[2,2048]{0,1:T(8,128)S(1)} %psum.37), channel_id=1, replica_groups=mesh['cuts_0'=2,'cuts_1'=2,'mode_0'=4,'mode_1'=4,'mode_2'=8] {'mode_1'}, use_global_device_ids=true, to_apply=%region_3.5 | all-reduce | flops 4096 | bytes 32768 | tf_op jit(solution)/shard_map/psum | solution.py:45
  606.6 58.6 %psum.39 = f32[2,2048]{0,1:T(8,128)S(1)} all-reduce(f32[2,2048]{0,1:T(8,128)S(1)} %psum.38), channel_id=1, replica_groups=mesh['cuts_0'=2,'cuts_1'=2,'mode_0'=4,'mode_1'=4,'mode_2'=8] {'mode_2'}, use_global_device_ids=true, to_apply=%region_4.6 | all-reduce | flops 4096 | bytes 32768 | tf_op jit(solution)/shard_map/psum | solution.py:45
  (33 shorter events, 6.7 us)
Async XLA Ops:
  7.2 103.9 %all-gather.12.cloned.1.call-start = ((), (), s32[]{:S(2)}) async-start(), calls=%async_computation.5 | async-start | bytes 1474560 | tf_op jit(solution)/shard_map/all_gather | solution.py:20
  41.6 143.6 %all-gather.8.cloned.1.call-start = ((), (), s32[]{:S(2)}) async-start(), calls=%async_computation.3 | async-start | bytes 5898240 | tf_op jit(solution)/shard_map/all_gather | solution.py:20
  83.6 168.4 %all-gather.10.cloned.1.call-start = ((), (), s32[]{:S(2)}) async-start(), calls=%async_computation.4 | async-start | bytes 5308416 | tf_op jit(solution)/shard_map/all_gather | solution.py:20
  111.0 197.3 %all-gather.14.cloned.1.call-start = ((), (), s32[]{:S(2)}) async-start(), calls=%async_computation.6 | async-start | bytes 5898240 | tf_op jit(solution)/shard_map/all_gather | solution.py:20
  122.3 199.7 %all-to-all-start = ((bf16[2,128,8,128]{3,2,0,1:T(8,128)(2,1)}), bf16[2,128,8,128]{3,2,0,1:T(8,128)(2,1)S(1)}, u32[]{:S(2)}, u32[]{:S(2)}) async-start(bf16[2,128,8,128]{3,2,0,1:T(8,128)(2,1)} %copy.45), calls=%async_computation | async-start | bytes 1048576 | tf_op jit(solution)/shard_map/all_to_all | solution.py:69
  331.2 70.8 %copy-start = (s32[2048]{0:T(1024)S(1)}, s32[2048]{0:T(1024)}, u32[]{:S(2)}) copy-start(s32[2048]{0:T(1024)} %param.13) | copy-start | bytes 24580
  331.2 70.8 %copy-start.1 = (s32[2048]{0:T(1024)S(1)}, s32[2048]{0:T(1024)}, u32[]{:S(2)}) copy-start(s32[2048]{0:T(1024)} %param.12) | copy-start | bytes 24580
  340.2 32.7 %all-to-all-start.1 = ((bf16[2,128,8,128]{3,2,0,1:T(8,128)(2,1)}), bf16[2,128,8,128]{3,2,0,1:T(8,128)(2,1)S(1)}, u32[]{:S(2)}, u32[]{:S(2)}) async-start(bf16[2,128,8,128]{3,2,0,1:T(8,128)(2,1)} %copy.49), calls=%async_computation.1 | async-start | bytes 1048576 | tf_op jit(solution)/shard_map/all_to_all | solution.py:69
  391.0 25.8 %all-to-all-start.2 = ((bf16[2,128,8,128]{3,2,0,1:T(8,128)(2,1)}), bf16[2,128,8,128]{3,2,0,1:T(8,128)(2,1)S(1)}, u32[]{:S(2)}, u32[]{:S(2)}) async-start(bf16[2,128,8,128]{3,2,0,1:T(8,128)(2,1)} %copy.53), calls=%async_computation.2 | async-start | bytes 1048576 | tf_op jit(solution)/shard_map/all_to_all | solution.py:69
Sparse Core Ops, SparseCore 0:
  41.7 36.6 all-gather.11
  83.7 101.3 all-gather.7
  187.2 64.7 all-gather.9
  254.0 54.2 all-gather.13
where the time goes:
time: 673 us; the launch traced here: 672 us
  blocking collectives  296 us (44%)
  waiting for transfers between devices  191 us (28%)
  local copies, waits for them, and re-layouts  74 us (11%)
  starting transfers between devices  35.9 us (5%)
  other arithmetic  27.9 us (4%)
  matrix products  27.6 us (4%)
  between operations  19.9 us (3%)
    psum x5, blocking collectives, over_axes(): shard = lax.psum(shard, axis)  194 us
    all_gather x4, waiting for transfers between devices, gather_in_order(): blocks = lax.all_gather(blocks, axes[k], axis=0, tiled=True)  161 us
    all_gather x5, blocking collectives, gather_in_order(): blocks = lax.all_gather(blocks, axes[k], axis=0, tiled=True)  102 us
    all_to_all x3, starting transfers between devices, body(): lax.all_to_all(view, MODE, split_axis=1, concat_axis=1, tiled=True)  35.8 us
    all_to_all x3, waiting for transfers between devices, body(): lax.all_to_all(view, MODE, split_axis=1, concat_axis=1, tiled=True)  29.6 us
    dot_general x12, matrix products, product(): lax.dot_general(left, right, numbers, preferred_element_type=jnp.float32)  27.6 us
    another operation x4, local copies, waits for them, and re-layouts, absorb(): return jnp.stack([real, imag], axis=0)  22.1 us
    gather x1, local copies, waits for them, and re-layouts, body(): values = jnp.take(flat, flat_index, axis=1).astype(jnp.float32)  21.5 us
  transfers between devices with their start and end apart: 7, of which 5 were waited for; matrix products, arithmetic and copies ran while one was open for 6% of the time, Pallas kernels for 0%

commit v1 on v0

v1 whole, which is shorter than its diff:
```python
import functools

import jax
import jax.numpy as jnp
from jax import lax
from jax.experimental import pallas as pl
from jax.experimental.pallas import tpu as pltpu
from jax.sharding import PartitionSpec as P

MESH = pl.DeviceIdType.MESH
BF = jnp.bfloat16
F32 = jnp.float32
SIZE = {"x": 4, "y": 4, "z": 8}
ORDERS = ("xyz", "yzx", "zxy")
LANES = (
    ((0, 256), (256, 128), (384, 128)),
    ((0, 128), (128, 256), (384, 128)),
    ((0, 128), (128, 128), (256, 256)),
)
LAG = 2


def kernel(order, stem, br, idx, rb, cb, out, amp, MT, Y, X, S, Y3T, snd1, rcv1, snd2, rcv2, a0, a1, a2, a3, a4,
           s_a2a, r_a2a, s_ag, r_ag, s_p, r_p, s_am, r_am):
    c = lax.axis_index("cuts")
    m = lax.axis_index("mode")
    core, yh = c % 2, c // 2
    me = {"x": m // 32, "y": (m // 8) % 4, "z": m % 8}
    yg = yh * 4 + me["y"]

    def mode_of(x, y, z):
        return x * 32 + y * 8 + z

    def near(d, step):
        if d == "x":
            return c, mode_of((me["x"] + step + 4) % 4, me["y"], me["z"])
        if d == "z":
            return c, mode_of(me["x"], me["y"], (me["z"] + step + 8) % 8)
        g = (yg + step + 8) % 8
        return (g // 4) * 2 + core, mode_of(me["x"], g % 4, me["z"])

    def far(i):
        k = (i * 37) % 128
        return mode_of((me["x"] + k // 32) % 4, (me["y"] + (k // 8) % 4) % 4, (me["z"] + k % 8) % 8)

    barrier = pltpu.get_barrier_semaphore()

    def greet(i, carry):
        pl.semaphore_signal(barrier, inc=1, device_id=(c, far(i)), device_id_type=MESH)
        return carry

    lax.fori_loop(1, 128, greet, 0)
    for k in range(1, 4):
        pl.semaphore_signal(barrier, inc=1, device_id=((c + k) % 4, m), device_id_type=MESH)
    for k in (-1, 1):
        pl.semaphore_signal(barrier, inc=1, device_id=near("y", k), device_id_type=MESH)

    for t in range(3):
        mine = br[order[t]]
        MT[t, core, me["x"], me["y"], me["z"]] = jnp.where(core == 0, mine[:, :512], mine[:, 512:])

    lane = lax.broadcasted_iota(jnp.int32, (128, 1024), 1)

    def permute(t, put):
        for k in range(8):
            hot = (lane == idx[t, :, k : k + 1]).astype(F32).astype(BF)
            z = jnp.dot(hot, Y[...], preferred_element_type=F32)
            put(k, 0, z[:, :128].T)
            put(k, 1, z[:, 128:].T)

    Y[:, :128] = stem[0]
    Y[:, 128:] = stem[1]

    def put_send(k, p, block):
        S[pl.ds(p * 8 + k, 128, stride=16), :] = block

    permute(0, put_send)
    snd1[...] = S[...].reshape(128, 16, 128).astype(BF)
    pl.semaphore_wait(barrier, 132)

    def exchange(send, recv, n):
        def go(i, carry):
            peer = far(i)
            pltpu.make_async_remote_copy(
                src_ref=send.at[peer], dst_ref=recv.at[m], send_sem=s_a2a.at[n], recv_sem=r_a2a.at[n],
                device_id=(c, peer), device_id_type=MESH,
            ).start()
            return carry

        lax.fori_loop(1, 128, go, 0)
        recv[m] = send[m]

    def exchange_wait(send, recv, n):
        copy = pltpu.make_async_remote_copy(
            src_ref=send.at[pl.ds(0, 127)], dst_ref=recv.at[pl.ds(0, 127)], send_sem=s_a2a.at[n], recv_sem=r_a2a.at[n],
            device_id=(c, far(1)), device_id_type=MESH,
        )
        copy.wait_send()
        copy.wait_recv()

    partner = (yh * 2 + 1 - core, m)

    def share(t, region):
        pltpu.make_async_remote_copy(
            src_ref=region, dst_ref=region, send_sem=s_p.at[t], recv_sem=r_p.at[t], device_id=partner, device_id_type=MESH
        ).start()

    def gather_steps(t, kind):
        start, width = LANES[t][kind]
        item = t * 3 + kind
        dims = ORDERS[kind]
        steps = []
        count = [0]
        waiting = []
        sent = []

        def region(ph, q, half=None):
            at = []
            for d in "xyz":
                place = dims.index(d)
                if place < ph:
                    if half is not None and place == ph - 1:
                        at.append(pl.ds(half * (SIZE[d] // 2), SIZE[d] // 2))
                    else:
                        at.append(pl.ds(0, SIZE[d]))
                elif place == ph:
                    at.append(q)
                else:
                    at.append(me[d])
            return MT.at[t, core, at[0], at[1], at[2], :, pl.ds(start, width)]

        def hop(d, step, src, landing):
            k = count[0]
            count[0] += 1
            copy = pltpu.make_async_remote_copy(
                src_ref=src, dst_ref=src, send_sem=s_ag.at[item, k], recv_sem=r_ag.at[item, k],
                device_id=near(d, step), device_id_type=MESH,
            )
            arrive = pltpu.make_async_remote_copy(
                src_ref=landing, dst_ref=landing, send_sem=s_ag.at[item, k], recv_sem=r_ag.at[item, k],
                device_id=near(d, step), device_id_type=MESH,
            )
            copy.start()
            sent.append(copy)
            waiting.append((arrive, landing))

        def settle(last):
            for arrive, landing in waiting:
                arrive.wait_recv()
                if last:
                    share(t, landing)
            waiting.clear()

        def make(ph, s):
            d = dims[ph]
            n = SIZE[d]
            q = me[d]
            top = n // 2 - 1

            def at(k):
                return (q + k + n) % n

            def step():
                settle(ph == 2 and s > 0)
                if ph == 2 and s == 0:
                    share(t, region(2, q))
                if s < top:
                    hop(d, 1, region(ph, at(-s)), region(ph, at(-s - 1)))
                    hop(d, -1, region(ph, at(s)), region(ph, at(s + 1)))
                elif ph == 0:
                    hop(d, 1, region(ph, at(-s)), region(ph, at(-s - 1)))
                else:
                    hop(d, 1, region(ph, at(-s), 0), region(ph, at(-s - 1), 0))
                    hop(d, -1, region(ph, at(s), 1), region(ph, at(s + 1), 1))

            return step

        for ph in range(3):
            for s in range(SIZE[dims[ph]] // 2):
                steps.append(make(ph, s))
        steps.append(lambda: settle(True))

        def finish():
            for copy in sent:
                copy.wait_send()

        return steps, finish

    items = [[gather_steps(t, kind) for kind in range(3)] for t in range(3)]
    n_steps = len(items[0][0][0])

    exchange(snd1, rcv1, 0)
    for turn in range(n_steps + 2 * LAG):
        for t in range(3):
            s = turn - t * LAG
            if 0 <= s < n_steps:
                for kind in range(3):
                    items[t][kind][0][s]()

    def share_wait(t):
        copy = pltpu.make_async_remote_copy(
            src_ref=MT.at[t, core], dst_ref=MT.at[t, 1 - core], send_sem=s_p.at[t], recv_sem=r_p.at[t],
            device_id=partner, device_id_type=MESH,
        )
        copy.wait_send()
        copy.wait_recv()

    def absorb(t):
        def part(g, carry):
            gx, gy = g // 2, g % 2
            low = MT[t, 0, gx, pl.ds(gy * 2, 2)].reshape(256, 512)
            high = MT[t, 1, gx, pl.ds(gy * 2, 2)].reshape(256, 512)
            o = jnp.dot(low, X[:512], preferred_element_type=F32) + jnp.dot(high, X[512:], preferred_element_type=F32)
            o = o.reshape(16, 16, 256)
            re = o[:, :8, :128] - o[:, 8:, 128:]
            im = o[:, :8, 128:] + o[:, 8:, :128]
            rows = pl.ds(pl.multiple_of(g * 128, 128), 128)
            Y[rows, :128] = re.reshape(128, 128).astype(BF)
            Y[rows, 128:] = im.reshape(128, 128).astype(BF)
            return carry

        lax.fori_loop(0, 8, part, 0)

    exchange_wait(snd1, rcv1, 0)
    first = rcv1[...].astype(F32)
    X[:, :128] = first[:, :8, :].reshape(1024, 128).astype(BF)
    X[:, 128:] = first[:, 8:, :].reshape(1024, 128).astype(BF)

    def put_next(k, p, block):
        S[pl.ds(p * 1024 + k, 128, stride=8), :] = block

    for t in range(3):
        if t > 0:
            permute(t, put_next)
            X[:, :128] = S[:1024].astype(BF)
            X[:, 128:] = S[1024:].astype(BF)
        share_wait(t)
        absorb(t)

    for p in range(2):
        for j in range(8):
            block = Y[j * 128 : (j + 1) * 128, p * 128 : (p + 1) * 128].astype(F32).T
            S[pl.ds(p * 8 + j, 128, stride=16), :] = block
            Y3T[p * 128 : (p + 1) * 128, j * 128 : (j + 1) * 128] = block.astype(BF)
    snd2[...] = S[...].reshape(128, 16, 128).astype(BF)
    exchange(snd2, rcv2, 1)

    state = lax.broadcasted_iota(jnp.int32, (1024, 512), 0)
    place = lax.broadcasted_iota(jnp.int32, (128, 512), 0)
    for q in range(4):
        rows = rb[:, q * 512 : (q + 1) * 512]
        cols = cb[:, q * 512 : (q + 1) * 512]
        hot = (state == rows).astype(F32).astype(BF)
        got = jnp.dot(Y3T[...], hot, preferred_element_type=F32)
        here = (place == cols // 128) & (cols % 128 == m)
        for p in range(2):
            val = jnp.sum(jnp.where(here, got[p * 128 : (p + 1) * 128], 0.0), axis=0, keepdims=True)
            a0[q, p : p + 1, :] = val

    def spread(src_of, buf, peers, mine, n):
        copies = []
        for k, peer in enumerate(peers):
            copy = pltpu.make_async_remote_copy(
                src_ref=src_of(k), dst_ref=buf.at[k + 1], send_sem=s_am.at[n, k], recv_sem=r_am.at[n, k],
                device_id=peer, device_id_type=MESH,
            )
            copy.start()
            copies.append(copy)
        buf[0] = mine
        for copy in copies:
            copy.wait()
        total = buf[0]
        for k in range(len(peers)):
            total = total + buf[k + 1]
        return total

    t1 = spread(lambda k: a0.at[(c + k + 1) % 4], a1, [((c + k) % 4, m) for k in range(1, 4)], a0[c], 0)
    for g in range(4):
        a2[g, :, :] = t1[:, g * 128 : (g + 1) * 128]
    mx = me["x"]
    t2 = spread(
        lambda k: a2.at[(mx + k + 1) % 4], a3,
        [(c, mode_of((mx + k) % 4, me["y"], me["z"])) for k in range(1, 4)], a2[mx], 1,
    )
    a2[4] = t2
    t3 = spread(
        lambda k: a2.at[4], a3.at[pl.ds(4, 4)],
        [(c, mode_of(mx, (me["y"] + k) % 4, me["z"])) for k in range(1, 4)], t2, 2,
    )
    a2[5] = t3
    t4 = spread(
        lambda k: a2.at[5], a4,
        [(c, mode_of(mx, me["y"], (me["z"] + k) % 8)) for k in range(1, 8)], t3, 3,
    )
    amp[...] = t4

    for t in range(3):
        for kind in range(3):
            items[t][kind][1]()
    exchange_wait(snd2, rcv2, 1)
    S[...] = rcv2[...].astype(F32).reshape(2048, 128)
    for p in range(2):
        for j in range(8):
            block = S[pl.ds(p * 8 + j, 128, stride=16), :]
            out[p, j * 128 : (j + 1) * 128, :] = block.T.astype(BF)


def body(stem, branches, order, swap_order, row_bits, column_bits):
    vmem = pl.BlockSpec(memory_space=pltpu.VMEM)
    br = branches.transpose(0, 1, 3, 2).reshape(3, 16, 1024)
    idx = swap_order.reshape(3, 128, 8)
    dma = pltpu.SemaphoreType.DMA
    field, amps = pl.pallas_call(
        kernel,
        out_shape=(jax.ShapeDtypeStruct((2, 1024, 128), BF), jax.ShapeDtypeStruct((2, 128), F32)),
        in_specs=[pl.BlockSpec(memory_space=pltpu.SMEM)] + [vmem] * 5,
        out_specs=(vmem, vmem),
        scratch_shapes=[
            pltpu.VMEM((3, 2, 4, 4, 8, 16, 512), BF),
            pltpu.VMEM((1024, 256), BF),
            pltpu.VMEM((1024, 256), BF),
            pltpu.VMEM((2048, 128), F32),
            pltpu.VMEM((256, 1024), BF),
            pltpu.VMEM((128, 16, 128), BF),
            pltpu.VMEM((128, 16, 128), BF),
            pltpu.VMEM((128, 16, 128), BF),
            pltpu.VMEM((128, 16, 128), BF),
            pltpu.VMEM((4, 2, 512), F32),
            pltpu.VMEM((4, 2, 512), F32),
            pltpu.VMEM((6, 2, 128), F32),
            pltpu.VMEM((8, 2, 128), F32),
            pltpu.VMEM((8, 2, 128), F32),
            dma((2,)), dma((2,)),
            dma((9, 16)), dma((9, 16)),
            dma((3,)), dma((3,)),
            dma((4, 7)), dma((4, 7)),
        ],
        compiler_params=pltpu.CompilerParams(collective_id=0, has_side_effects=True, vmem_limit_bytes=48 * 1024 * 1024),
    )(order, stem[0], br, idx, row_bits.reshape(1, 2048), column_bits.reshape(1, 2048))
    m = lax.axis_index("mode")
    amps = lax.dynamic_slice_in_dim(amps, (m % 32) * 4, 4, 1)
    return field[None], amps


def solution(mesh):
    placed = (P("cuts", None, None, "mode"), P(None, None, None, "mode"), P(), P(), P(), P())
    return jax.shard_map(
        body,
        mesh=mesh,
        in_specs=placed,
        out_specs=(P("cuts", None, None, "mode"), P(None, ("cuts", "mode"))),
        check_vma=False,
    )
```

time: 673 us -> 127 us (0.19)
  blocking collectives: 296 us -> 0 us
  waiting for transfers between devices: 191 us -> 0 us
  Pallas kernels: 0 us -> 122 us
  local copies, waits for them, and re-layouts: 74 us -> 4.05 us
  starting transfers between devices: 35.9 us -> 0 us
  other arithmetic: 27.9 us -> 0 us
  matrix products: 27.6 us -> 0 us
  between operations: 19.9 us -> 0.69 us
    psum x5 -> x0, blocking collectives: 194 us -> none  [over_axes(): shard = lax.psum(shard, axis)]
    all_gather x4 -> x0, waiting for transfers between devices: 161 us -> none  [gather_in_order(): blocks = lax.all_gather(blocks, axes[k], axis=0, tiled=True)]
    pallas_call x0 -> x1, Pallas kernels: none -> 122 us  [body(): pl.pallas_call(kernel, out_shape=(jax.ShapeDtypeStruct((2, 1024, 128), BF...]
    all_gather x5 -> x0, blocking collectives: 102 us -> none  [gather_in_order(): blocks = lax.all_gather(blocks, axes[k], axis=0, tiled=True)]
    all_to_all x3 -> x0, starting transfers between devices: 35.8 us -> none  [body(): lax.all_to_all(view, MODE, split_axis=1, concat_axis=1, tiled=True)]
    gather x4 -> x0, local copies, waits for them, and re-layouts: 32.6 us -> none  [the longest x1 21.5 us: body(): values = jnp.take(flat, flat_index, axis=1).astype(jnp.float32)]
    all_to_all x3 -> x0, waiting for transfers between devices: 29.6 us -> none  [body(): lax.all_to_all(view, MODE, split_axis=1, concat_axis=1, tiled=True)]
    dot_general x12 -> x0, matrix products: 27.6 us -> none  [product(): lax.dot_general(left, right, numbers, preferred_element_type=jnp.float32)]
  transfers between devices with their start and end apart: 7 -> 0, of which waited for: 5 -> 0; matrix products, arithmetic and copies ran while one was open for 6% -> 0% of each run, Pallas kernels for 0% -> 0%
where the time goes in v1:
time: 127 us; the launch traced here: 126 us
  Pallas kernels  122 us (96%)
  local copies, waits for them, and re-layouts  4.05 us (3%)
    pallas_call x1, Pallas kernels, body(): pl.pallas_call(kernel, out_shape=(jax.ShapeDtypeStruct((2, 1024, 128), BF...  122 us
    unnamed x13, local copies, waits for them, and re-layouts  3.28 us

profile of v1, /device:TPU:6, one launch (start us, length us, event | category | flops | bytes accessed | tf_op | source)
XLA Modules:
  0.0 126.4 jit_solution(11336096197963394288)
XLA Ops:
  0.6 0.0 copy-start.5
  0.7 0.7 copy-done.5
  1.4 0.0 copy-start.1
  1.4 0.0 copy-start.2
  1.4 0.0 copy-start.3
  1.4 0.1 reshape.17.idx
  1.5 0.0 copy-start.4
  1.5 0.7 copy-done.1
  2.2 0.0 copy-done.2
  2.2 0.0 copy-done.3
  2.2 0.0 copy-done.4
  2.3 0.0 copy-start
  2.3 1.0 copy-done
  3.3 121.6 %shard_map.77 = (bf16[2,1024,128]{2,1,0:T(8,128)(2,1)S(1)}, f32[2,128]{1,0:T(2,128)S(1)}) custom-call(s32[3]{0:T(128)S(1)} %copy-done.4, bf16[2,1024,128]{2,1,0:T(8,128)(2,1)S(1)} %bitcast.7, bf16[3,16,1024]{2,1,0:T(8,128)(2,1)S(1)} %bitcast.9, s32[3,128,8]{2,1,0:T(8,128)S(1)} %reshape.17.idx, s32[1,2048]{1,0:T(1,128)S(1)} %bitcast.10, s32[1,2048]{1,0:T(1,128)S(1)} %bitcast.11), custom_call_target="tpu_custom_call" | custom-call | tf_op jit(solution)/shard_map/pallas_call | solution.py:313
  124.9 0.6 constant_dynamic-slice_fusion
  125.6 0.8 copy.9
Async XLA Ops:
  0.6 0.7 copy-start.5
  1.4 0.9 copy-start.1
  1.4 0.9 copy-start.2
  1.4 0.9 copy-start.3
  1.5 0.8 copy-start.4
  2.3 1.0 copy-start

commit v2 on v1

--- a/solution.py
+++ b/solution.py
@@ -11,17 +11,15 @@
 BF = jnp.bfloat16
 F32 = jnp.float32
 SIZE = {"x": 4, "y": 4, "z": 8}
-ORDERS = ("xyz", "yzx", "zxy")
-LANES = (
-    ((0, 256), (256, 128), (384, 128)),
-    ((0, 128), (128, 256), (384, 128)),
-    ((0, 128), (128, 128), (256, 256)),
-)
-LAG = 2
-
-
-def kernel(order, stem, br, idx, rb, cb, out, amp, MT, Y, X, S, Y3T, snd1, rcv1, snd2, rcv2, a0, a1, a2, a3, a4,
-           s_a2a, r_a2a, s_ag, r_ag, s_p, r_p, s_am, r_am):
+ORDERS = ("xyz", "zyx", "zxy")
+DIRECT = ((0, 1), (0,), (0,))
+HALF = (("", "", "x"), ("", "z", "y"), ("", "z", "x"))
+TILES = (((0, 2), (2, 1)), ((0, 1), (1, 2)), ((0, 2), (2, 1)))
+LAG = 0
+
+
+def kernel(order, stem_h, br_h, idx, rb, cb, out, amp, stem, br, MA, MB, Y, X, S, Y3T, snd1, rcv1, snd2, rcv2, a0, a1, a2, a3, a4,
+           s_a2a, r_a2a, s_ag, r_ag, s_p, r_p, s_am, r_am, s_in, plane, cube):
     c = lax.axis_index("cuts")
     m = lax.axis_index("mode")
     core, yh = c % 2, c // 2
@@ -43,21 +41,29 @@
         k = (i * 37) % 128
         return mode_of((me["x"] + k // 32) % 4, (me["y"] + (k // 8) % 4) % 4, (me["z"] + k % 8) % 8)
 
+    get_stem = pltpu.make_async_copy(stem_h, stem, s_in.at[0])
+    get_br = pltpu.make_async_copy(br_h, br, s_in.at[1])
+    get_br.start()
+    get_stem.start()
     barrier = pltpu.get_barrier_semaphore()
-
-    def greet(i, carry):
-        pl.semaphore_signal(barrier, inc=1, device_id=(c, far(i)), device_id_type=MESH)
-        return carry
-
-    lax.fori_loop(1, 128, greet, 0)
-    for k in range(1, 4):
-        pl.semaphore_signal(barrier, inc=1, device_id=((c + k) % 4, m), device_id_type=MESH)
-    for k in (-1, 1):
-        pl.semaphore_signal(barrier, inc=1, device_id=near("y", k), device_id_type=MESH)
-
+    line_x = [(c, mode_of((me["x"] + k) % 4, me["y"], me["z"])) for k in range(1, 4)]
+    line_y = [(c, mode_of(me["x"], (me["y"] + k) % 4, me["z"])) for k in range(1, 4)]
+    line_z = [(c, mode_of(me["x"], me["y"], (me["z"] + k) % 8)) for k in range(1, 8)]
+    cuts = [((c + k) % 4, m) for k in range(1, 4)]
+
+    def tell(sem, peers):
+        for peer in peers:
+            pl.semaphore_signal(sem, inc=1, device_id=peer, device_id_type=MESH)
+
+    tell(barrier, line_x + line_y + line_z + cuts + [near("y", -1), near("y", 1), near("y", -2)])
+
+    get_br.wait()
     for t in range(3):
         mine = br[order[t]]
-        MT[t, core, me["x"], me["y"], me["z"]] = jnp.where(core == 0, mine[:, :512], mine[:, 512:])
+        mine = jnp.where(core == 0, mine[:, :512], mine[:, 512:])
+        MA[t, core, me["z"], me["x"], me["y"]] = mine[:, :128]
+        for u in range(3):
+            MB[t, core, u, me["x"], me["y"], me["z"]] = mine[:, 128 * (u + 1) : 128 * (u + 2)]
 
     lane = lax.broadcasted_iota(jnp.int32, (128, 1024), 1)
 
@@ -68,17 +74,10 @@
             put(k, 0, z[:, :128].T)
             put(k, 1, z[:, 128:].T)
 
-    Y[:, :128] = stem[0]
-    Y[:, 128:] = stem[1]
-
     def put_send(k, p, block):
         S[pl.ds(p * 8 + k, 128, stride=16), :] = block
 
-    permute(0, put_send)
-    snd1[...] = S[...].reshape(128, 16, 128).astype(BF)
-    pl.semaphore_wait(barrier, 132)
-
-    def exchange(send, recv, n):
+    def exchange(send, recv, n, lo=1, hi=128):
         def go(i, carry):
             peer = far(i)
             pltpu.make_async_remote_copy(
@@ -87,8 +86,7 @@
             ).start()
             return carry
 
-        lax.fori_loop(1, 128, go, 0)
-        recv[m] = send[m]
+        lax.fori_loop(lo, hi, go, 0)
 
     def exchange_wait(send, recv, n):
         copy = pltpu.make_async_remote_copy(
@@ -100,13 +98,13 @@
 
     partner = (yh * 2 + 1 - core, m)
 
-    def share(t, region):
+    def share(t, kind, region):
         pltpu.make_async_remote_copy(
-            src_ref=region, dst_ref=region, send_sem=s_p.at[t], recv_sem=r_p.at[t], device_id=partner, device_id_type=MESH
+            src_ref=region, dst_ref=region, send_sem=s_p.at[t, min(kind, 1)], recv_sem=r_p.at[t, min(kind, 1)],
+            device_id=partner, device_id_type=MESH,
         ).start()
 
     def gather_steps(t, kind):
-        start, width = LANES[t][kind]
         item = t * 3 + kind
         dims = ORDERS[kind]
         steps = []
@@ -115,40 +113,53 @@
         sent = []
 
         def region(ph, q, half=None):
-            at = []
+            at = {}
             for d in "xyz":
                 place = dims.index(d)
                 if place < ph:
-                    if half is not None and place == ph - 1:
-                        at.append(pl.ds(half * (SIZE[d] // 2), SIZE[d] // 2))
+                    if half is not None and d == HALF[kind][ph]:
+                        at[d] = pl.ds(half * (SIZE[d] // 2), SIZE[d] // 2)
                     else:
-                        at.append(pl.ds(0, SIZE[d]))
+                        at[d] = pl.ds(0, SIZE[d])
                 elif place == ph:
-                    at.append(q)
+                    at[d] = q
                 else:
-                    at.append(me[d])
-            return MT.at[t, core, at[0], at[1], at[2], :, pl.ds(start, width)]
+                    at[d] = me[d]
+            if kind == 0:
+                return MA.at[t, core, at["z"], at["x"], at["y"]]
+            return MB.at[t, core, pl.ds(*TILES[t][kind - 1]), at["x"], at["y"], at["z"]]
+
+        def copy_of(ref, k, peer):
+            return pltpu.make_async_remote_copy(
+                src_ref=ref, dst_ref=ref, send_sem=s_ag.at[item, k], recv_sem=r_ag.at[item, k],
+                device_id=peer, device_id_type=MESH,
+            )
 
         def hop(d, step, src, landing):
             k = count[0]
             count[0] += 1
-            copy = pltpu.make_async_remote_copy(
-                src_ref=src, dst_ref=src, send_sem=s_ag.at[item, k], recv_sem=r_ag.at[item, k],
-                device_id=near(d, step), device_id_type=MESH,
-            )
-            arrive = pltpu.make_async_remote_copy(
-                src_ref=landing, dst_ref=landing, send_sem=s_ag.at[item, k], recv_sem=r_ag.at[item, k],
-                device_id=near(d, step), device_id_type=MESH,
-            )
+            copy = copy_of(src, k, near(d, step))
             copy.start()
             sent.append(copy)
-            waiting.append((arrive, landing))
+            waiting.append((copy_of(landing, k, near(d, step)), landing))
+
+        def direct(ph):
+            d = dims[ph]
+            k = count[0]
+            count[0] += 1
+            src = region(ph, me[d])
+            for step in {"x": (1, 2, 3), "y": (1, -1, 2), "z": (1, 7, 2, 6, 3, 5, 4)}[d]:
+                copy_of(src, k, near(d, step)).start()
+            landing = region(ph, pl.ds(0, SIZE[d] - 1))
+            arrive = copy_of(landing, k, near(d, 1))
+            sent.append(arrive)
+            waiting.append((arrive, None))
 
         def settle(last):
             for arrive, landing in waiting:
                 arrive.wait_recv()
                 if last:
-                    share(t, landing)
+                    share(t, kind, landing)
             waiting.clear()
 
         def make(ph, s):
@@ -163,12 +174,12 @@
             def step():
                 settle(ph == 2 and s > 0)
                 if ph == 2 and s == 0:
-                    share(t, region(2, q))
-                if s < top:
+                    share(t, kind, region(2, q))
+                if ph in DIRECT[kind]:
+                    direct(ph)
+                elif s < top:
                     hop(d, 1, region(ph, at(-s)), region(ph, at(-s - 1)))
                     hop(d, -1, region(ph, at(s)), region(ph, at(s + 1)))
-                elif ph == 0:
-                    hop(d, 1, region(ph, at(-s)), region(ph, at(-s - 1)))
                 else:
                     hop(d, 1, region(ph, at(-s), 0), region(ph, at(-s - 1), 0))
                     hop(d, -1, region(ph, at(s), 1), region(ph, at(s + 1), 1))
@@ -176,7 +187,7 @@
             return step
 
         for ph in range(3):
-            for s in range(SIZE[dims[ph]] // 2):
+            for s in range(1 if ph in DIRECT[kind] else SIZE[dims[ph]] // 2):
                 steps.append(make(ph, s))
         steps.append(lambda: settle(True))
 
@@ -187,30 +198,53 @@
         return steps, finish
 
     items = [[gather_steps(t, kind) for kind in range(3)] for t in range(3)]
-    n_steps = len(items[0][0][0])
-
-    exchange(snd1, rcv1, 0)
-    for turn in range(n_steps + 2 * LAG):
+    def gather_turn(turn):
         for t in range(3):
-            s = turn - t * LAG
-            if 0 <= s < n_steps:
-                for kind in range(3):
-                    items[t][kind][0][s]()
+            for kind in range(3):
+                steps = items[t][kind][0]
+                s = turn - t * LAG
+                if 0 <= s < len(steps):
+                    steps[s]()
+
+    n_turns = max(len(it[0]) for row in items for it in row) + 2 * LAG
 
     def share_wait(t):
-        copy = pltpu.make_async_remote_copy(
-            src_ref=MT.at[t, core], dst_ref=MT.at[t, 1 - core], send_sem=s_p.at[t], recv_sem=r_p.at[t],
-            device_id=partner, device_id_type=MESH,
-        )
-        copy.wait_send()
-        copy.wait_recv()
+        for n, buf in enumerate((MA, MB)):
+            copy = pltpu.make_async_remote_copy(
+                src_ref=buf.at[t, core], dst_ref=buf.at[t, 1 - core], send_sem=s_p.at[t, n], recv_sem=r_p.at[t, n],
+                device_id=partner, device_id_type=MESH,
+            )
+            copy.wait_send()
+            copy.wait_recv()
+
+    pl.semaphore_wait(barrier, 19)
+    gather_turn(0)
+    tell(plane, line_y)
+    get_stem.wait()
+    Y[:, :128] = stem[0]
+    Y[:, 128:] = stem[1]
+    permute(0, put_send)
+    snd1[...] = S[...].reshape(128, 16, 128).astype(BF)
+    rcv1[m] = snd1[m]
+    pl.semaphore_wait(plane, 3)
+    tell(cube, line_x)
+    gather_turn(1)
+    pl.semaphore_wait(cube, 3)
+    cut = [1, 33, 65, 97, 128]
+    for turn in range(2, n_turns):
+        if turn - 2 < 4:
+            exchange(snd1, rcv1, 0, cut[turn - 2], cut[turn - 1])
+        gather_turn(turn)
 
     def absorb(t):
         def part(g, carry):
             gx, gy = g // 2, g % 2
-            low = MT[t, 0, gx, pl.ds(gy * 2, 2)].reshape(256, 512)
-            high = MT[t, 1, gx, pl.ds(gy * 2, 2)].reshape(256, 512)
-            o = jnp.dot(low, X[:512], preferred_element_type=F32) + jnp.dot(high, X[512:], preferred_element_type=F32)
+            o = None
+            for h in range(2):
+                tiles = [jnp.concatenate([MA[t, h, z, gx, gy * 2 + j] for j in range(2) for z in range(8)], axis=0)]
+                tiles += [MB[t, h, u, gx, pl.ds(gy * 2, 2)].reshape(256, 128) for u in range(3)]
+                part_o = jnp.dot(jnp.concatenate(tiles, axis=1), X[h * 512 : (h + 1) * 512], preferred_element_type=F32)
+                o = part_o if o is None else o + part_o
             o = o.reshape(16, 16, 256)
             re = o[:, :8, :128] - o[:, 8:, 128:]
             im = o[:, :8, 128:] + o[:, 8:, :128]
@@ -244,6 +278,7 @@
             Y3T[p * 128 : (p + 1) * 128, j * 128 : (j + 1) * 128] = block.astype(BF)
     snd2[...] = S[...].reshape(128, 16, 128).astype(BF)
     exchange(snd2, rcv2, 1)
+    rcv2[m] = snd2[m]
 
     state = lax.broadcasted_iota(jnp.int32, (1024, 512), 0)
     place = lax.broadcasted_iota(jnp.int32, (128, 512), 0)
@@ -274,23 +309,23 @@
             total = total + buf[k + 1]
         return total
 
-    t1 = spread(lambda k: a0.at[(c + k + 1) % 4], a1, [((c + k) % 4, m) for k in range(1, 4)], a0[c], 0)
+    t1 = spread(lambda k: a0.at[(c + k + 1) % 4], a1, cuts, a0[c], 0)
     for g in range(4):
         a2[g, :, :] = t1[:, g * 128 : (g + 1) * 128]
     mx = me["x"]
     t2 = spread(
         lambda k: a2.at[(mx + k + 1) % 4], a3,
-        [(c, mode_of((mx + k) % 4, me["y"], me["z"])) for k in range(1, 4)], a2[mx], 1,
+        line_x, a2[mx], 1,
     )
     a2[4] = t2
     t3 = spread(
         lambda k: a2.at[4], a3.at[pl.ds(4, 4)],
-        [(c, mode_of(mx, (me["y"] + k) % 4, me["z"])) for k in range(1, 4)], t2, 2,
+        line_y, t2, 2,
     )
     a2[5] = t3
     t4 = spread(
         lambda k: a2.at[5], a4,
-        [(c, mode_of(mx, me["y"], (me["z"] + k) % 8)) for k in range(1, 8)], t3, 3,
+        line_z, t3, 3,
     )
     amp[...] = t4
 
@@ -313,10 +348,13 @@
     field, amps = pl.pallas_call(
         kernel,
         out_shape=(jax.ShapeDtypeStruct((2, 1024, 128), BF), jax.ShapeDtypeStruct((2, 128), F32)),
-        in_specs=[pl.BlockSpec(memory_space=pltpu.SMEM)] + [vmem] * 5,
+        in_specs=[pl.BlockSpec(memory_space=pltpu.SMEM)] + [pl.BlockSpec(memory_space=pltpu.HBM)] * 2 + [vmem] * 3,
         out_specs=(vmem, vmem),
         scratch_shapes=[
-            pltpu.VMEM((3, 2, 4, 4, 8, 16, 512), BF),
+            pltpu.VMEM((2, 1024, 128), BF),
+            pltpu.VMEM((3, 16, 1024), BF),
+            pltpu.VMEM((3, 2, 8, 4, 4, 16, 128), BF),
+            pltpu.VMEM((3, 2, 3, 4, 4, 8, 16, 128), BF),
             pltpu.VMEM((1024, 256), BF),
             pltpu.VMEM((1024, 256), BF),
             pltpu.VMEM((2048, 128), F32),
@@ -331,9 +369,11 @@
             pltpu.VMEM((8, 2, 128), F32),
             pltpu.VMEM((8, 2, 128), F32),
             dma((2,)), dma((2,)),
-            dma((9, 16)), dma((9, 16)),
-            dma((3,)), dma((3,)),
+            dma((9, 12)), dma((9, 12)),
+            dma((3, 2)), dma((3, 2)),
             dma((4, 7)), dma((4, 7)),
+            dma((2,)),
+            pltpu.SemaphoreType.REGULAR, pltpu.SemaphoreType.REGULAR,
         ],
         compiler_params=pltpu.CompilerParams(collective_id=0, has_side_effects=True, vmem_limit_bytes=48 * 1024 * 1024),
     )(order, stem[0], br, idx, row_bits.reshape(1, 2048), column_bits.reshape(1, 2048))

time: 127 us -> 99.8 us (0.79)
  Pallas kernels: 122 us -> 94.7 us
    pallas_call x1, Pallas kernels: 122 us -> 94.7 us  [body(): pl.pallas_call(kernel, out_shape=(jax.ShapeDtypeStruct((2, 1024, 128), BF...]
where the time goes in v2:
time: 99.8 us; the launch traced here: 99.5 us
  Pallas kernels  94.7 us (95%)
  local copies, waits for them, and re-layouts  4.05 us (4%)
    pallas_call x1, Pallas kernels, body(): pl.pallas_call(kernel, out_shape=(jax.ShapeDtypeStruct((2, 1024, 128), BF...  94.7 us
    unnamed x13, local copies, waits for them, and re-layouts  3.28 us

profile of v2, /device:TPU:6, one launch (start us, length us, event | category | flops | bytes accessed | tf_op | source)
XLA Modules:
  0.0 99.5 jit_solution(16037951323662909212)
XLA Ops:
  0.6 0.0 copy-start.5
  0.7 0.7 copy-done.5
  1.4 0.0 copy-start.1
  1.4 0.0 copy-start.2
  1.4 0.0 copy-start.3
  1.4 0.1 reshape.17.idx
  1.5 0.0 copy-start.4
  1.5 0.7 copy-done.1
  2.2 0.0 copy-done.2
  2.2 0.0 copy-done.3
  2.2 0.0 copy-done.4
  2.3 0.0 copy-start
  2.3 1.0 %copy-done = bf16[1,2,1024,128]{3,2,1,0:T(8,128)(2,1)S(1)} copy-done((bf16[1,2,1024,128]{3,2,1,0:T(8,128)(2,1)S(1)}, bf16[1,2,1024,128]{3,2,1,0:T(8,128)(2,1)}, u32[]{:S(2)}) %copy-start) | copy-done | bytes 524312
  3.3 94.7 %shard_map.77 = (bf16[2,1024,128]{2,1,0:T(8,128)(2,1)S(1)}, f32[2,128]{1,0:T(2,128)S(1)}) custom-call(s32[3]{0:T(128)S(1)} %copy-done.4, bf16[2,1024,128]{2,1,0:T(8,128)(2,1)S(1)} %bitcast.7, bf16[3,16,1024]{2,1,0:T(8,128)(2,1)S(1)} %bitcast.9, s32[3,128,8]{2,1,0:T(8,128)S(1)} %reshape.17.idx, s32[1,2048]{1,0:T(1,128)S(1)} %bitcast.10, s32[1,2048]{1,0:T(1,128)S(1)} %bitcast.11), custom_call_target="tpu_custom_call" | custom-call | tf_op jit(solution)/shard_map/pallas_call | solution.py:348
  98.0 0.6 constant_dynamic-slice_fusion
  98.7 0.8 copy.9
Async XLA Ops:
  0.6 0.7 copy-start.5
  1.4 0.9 copy-start.1
  1.4 0.9 copy-start.2
  1.4 0.9 copy-start.3
  1.5 0.8 copy-start.4
  2.3 1.0 %copy-start = (bf16[1,2,1024,128]{3,2,1,0:T(8,128)(2,1)S(1)}, bf16[1,2,1024,128]{3,2,1,0:T(8,128)(2,1)}, u32[]{:S(2)}) copy-start(bf16[1,2,1024,128]{3,2,1,0:T(8,128)(2,1)} %param.6) | copy-start | bytes 1572868

commit v3 on v2

v3 whole, which is shorter than its diff:
```python
import functools

import jax
import jax.numpy as jnp
from jax import lax
from jax.experimental import pallas as pl
from jax.experimental.pallas import tpu as pltpu
from jax.sharding import PartitionSpec as P

MESH = pl.DeviceIdType.MESH
BF = jnp.bfloat16
F32 = jnp.float32
SIZE = {"x": 4, "y": 4, "z": 8}
ORDERS = ("xyz", "zyx", "zxy")
DIRECT = ((0, 1), (0,), (0,))
HALF = (("", "", "x"), ("", "z", "y"), ("", "z", "x"))
TILES = (((0, 0), (0, 2), (2, 2)), ((0, 2), (4, 1), (5, 1)), ((2, 1), (6, 2), (8, 1)))
RATE = 46.0
FLY = 2.0


def plan(tasks):
    now, free, done, ready_at, order = 0.0, {}, set(), {}, []
    left = list(tasks)
    while left:
        best = None
        for task in left:
            if any(dep not in ready_at for dep in task["deps"]):
                continue
            when = max([task["start"]] + [ready_at[dep] for dep in task["deps"]])
            score = (max(when, now), task["rank"])
            if best is None or score < best[0]:
                best = (score, task)
        (when, _), task = best
        left.remove(task)
        now = when + task["cost"]
        end = now
        for link, size in task["loads"].items():
            free[link] = max(free.get(link, 0.0), now) + size / RATE
            end = max(end, free[link])
        ready_at[task["key"]] = end + (FLY if task["loads"] else 0.0)
        order.append(task)
    return order


def kernel(order, stem_h, br_h, idx, rb, cb, out, amp, stem, br, MA, MB, PT, RT, Y, X, S, Y3T, snd1, rcv1, snd2, rcv2, a0, a1, a2, a3,
           s_a2a, r_a2a, s_ag, r_ag, s_p, r_p, s_am, r_am, s_in, plane, cube, square):
    c = lax.axis_index("cuts")
    m = lax.axis_index("mode")
    core, yh = c % 2, c // 2
    me = {"x": m // 32, "y": (m // 8) % 4, "z": m % 8}
    yg = yh * 4 + me["y"]

    def mode_of(x, y, z):
        return x * 32 + y * 8 + z

    def near(d, step):
        if d == "x":
            return c, mode_of((me["x"] + step + 4) % 4, me["y"], me["z"])
        if d == "z":
            return c, mode_of(me["x"], me["y"], (me["z"] + step + 8) % 8)
        g = (yg + step + 8) % 8
        return (g // 4) * 2 + core, mode_of(me["x"], g % 4, me["z"])

    def far(i):
        k = (i * 37) % 128
        return mode_of((me["x"] + k // 32) % 4, (me["y"] + (k // 8) % 4) % 4, (me["z"] + k % 8) % 8)

    get_stem = pltpu.make_async_copy(stem_h, stem, s_in.at[0])
    get_br = pltpu.make_async_copy(br_h, br, s_in.at[1])
    get_br.start()
    get_stem.start()
    barrier = pltpu.get_barrier_semaphore()
    line_x = [(c, mode_of((me["x"] + k) % 4, me["y"], me["z"])) for k in range(1, 4)]
    line_y = [(c, mode_of(me["x"], (me["y"] + k) % 4, me["z"])) for k in range(1, 4)]
    line_z = [(c, mode_of(me["x"], me["y"], (me["z"] + k) % 8)) for k in range(1, 8)]
    cuts = [((c + k) % 4, m) for k in range(1, 4)]

    def tell(sem, peers):
        for peer in peers:
            pl.semaphore_signal(sem, inc=1, device_id=peer, device_id_type=MESH)

    tell(barrier, line_x + line_y + line_z + cuts + [near("y", -1), near("y", 1), near("y", -2)])

    get_br.wait()
    for t in range(3):
        mine = br[order[t]]
        mine = jnp.where(core == 0, mine[:, :512], mine[:, 512:])
        u = 0
        for kind in range(3):
            for tile in range(TILES[t][kind][0], sum(TILES[t][kind])):
                part = mine[:, 128 * u : 128 * (u + 1)]
                u += 1
                if kind == 0:
                    MA[core, tile, me["z"], me["x"], me["y"]] = part
                else:
                    MB[core, tile, me["x"], me["y"], me["z"]] = part

    lane = lax.broadcasted_iota(jnp.int32, (128, 1024), 1)

    def table(t, k):
        return (lane == idx[t, :, k : k + 1]).astype(F32).astype(BF)

    def permute(t, put, ks):
        for k in ks:
            hot = table(t, k) if t == 0 else PT[t - 1, k * 128 : (k + 1) * 128, :]
            z = jnp.dot(hot, Y[...], preferred_element_type=F32)
            put(k, 0, z[:, :128].T)
            put(k, 1, z[:, 128:].T)

    state = lax.broadcasted_iota(jnp.int32, (1024, 256), 0)

    def make_pt(t, ks):
        for k in ks:
            PT[t - 1, k * 128 : (k + 1) * 128, :] = table(t, k)

    def make_rt(qs):
        for q in qs:
            RT[q] = (state == rb[:, q * 256 : (q + 1) * 256]).astype(F32).astype(BF)

    def put_send(k, p, block):
        S[pl.ds(p * 8 + k, 128, stride=16), :] = block

    def exchange(send, recv, n, lo=1, hi=128):
        def go(i, carry):
            peer = far(i)
            pltpu.make_async_remote_copy(
                src_ref=send.at[peer], dst_ref=recv.at[m], send_sem=s_a2a.at[n], recv_sem=r_a2a.at[n],
                device_id=(c, peer), device_id_type=MESH,
            ).start()
            return carry

        lax.fori_loop(lo, hi, go, 0)

    def exchange_wait(send, recv, n):
        copy = pltpu.make_async_remote_copy(
            src_ref=send.at[pl.ds(0, 127)], dst_ref=recv.at[pl.ds(0, 127)], send_sem=s_a2a.at[n], recv_sem=r_a2a.at[n],
            device_id=(c, far(1)), device_id_type=MESH,
        )
        copy.wait_send()
        copy.wait_recv()

    partner = (yh * 2 + 1 - core, m)

    def share(t, kind, region):
        pltpu.make_async_remote_copy(
            src_ref=region, dst_ref=region, send_sem=s_p.at[t, min(kind, 1)], recv_sem=r_p.at[t, min(kind, 1)],
            device_id=partner, device_id_type=MESH,
        ).start()

    tasks = []
    fns = {}
    seen = set()
    sent = []
    arrivals = {}

    def add(key, deps, fn, cost=0.08, loads=None, rank=0, start=0.0):
        tasks.append(dict(key=key, deps=deps, cost=cost, loads=loads or {}, rank=rank, start=start))
        fns[key] = fn

    def land(keys):
        for key in keys:
            if key in arrivals and key not in seen:
                seen.add(key)
                arrivals[key].wait_recv()

    def gather_item(t, kind):
        item = t * 3 + kind
        dims = ORDERS[kind]
        count = [0]
        width = TILES[t][kind][1]

        def region(ph, q, half=None):
            at = {}
            for d in "xyz":
                place = dims.index(d)
                if place < ph:
                    if half is not None and d == HALF[kind][ph]:
                        at[d] = pl.ds(half * (SIZE[d] // 2), SIZE[d] // 2)
                    else:
                        at[d] = pl.ds(0, SIZE[d])
                elif place == ph:
                    at[d] = q
                else:
                    at[d] = me[d]
            if kind == 0:
                return MA.at[core, pl.ds(*TILES[t][kind]), at["z"], at["x"], at["y"]]
            return MB.at[core, pl.ds(*TILES[t][kind]), at["x"], at["y"], at["z"]]

        def copy_of(ref, k, peer):
            return pltpu.make_async_remote_copy(
                src_ref=ref, dst_ref=ref, send_sem=s_ag.at[item, k], recv_sem=r_ag.at[item, k],
                device_id=peer, device_id_type=MESH,
            )

        def hop(ph, step, piece, half, deps, key):
            d = dims[ph]
            n = SIZE[d]
            k = count[0]
            count[0] += 1
            src = region(ph, (me[d] + piece + n) % n, half)
            landing = region(ph, (me[d] + piece - step + n) % n, half)
            arrivals[key] = copy_of(landing, k, near(d, step))
            size = 4 * width * (1 if half is None else 0.5)
            for done in dims[:ph]:
                size *= SIZE[done]

            def fn():
                land(deps)
                copy = copy_of(src, k, near(d, step))
                copy.start()
                sent.append(copy)

            add(key, deps, fn, loads={(d, step): size}, rank=t * 10 + ph)
            if ph == 2:

                def hand():
                    land([key])
                    share(t, kind, landing)

                add(key + ("share",), [key], hand, rank=t * 10 + 5, loads={("core", 1): size / 8})
            return key

        def direct(ph, deps, key):
            d = dims[ph]
            k = count[0]
            count[0] += 1
            src = region(ph, me[d])
            landing = region(ph, pl.ds(0, SIZE[d] - 1))
            arrivals[key] = copy_of(landing, k, near(d, 1))
            size = 4.0 * width * (1 if ph == 0 else 4) * {"x": 2, "y": 2, "z": 8}[d]

            def fn():
                land(deps)
                for step in {"x": (1, 2, 3), "y": (1, -1, 2), "z": (1, 7, 2, 6, 3, 5, 4)}[d]:
                    copy_of(src, k, near(d, step)).start()
                sent.append(arrivals[key])

            add(key, deps, fn, cost=0.3, loads={(d, 1): size, (d, -1): size}, rank=t * 10 + ph)
            return key

        def ring(ph, deps):
            d = dims[ph]
            tag = (t, kind, ph)
            out = []
            if SIZE[d] == 8:
                r, l = deps, deps
                for s in range(3):
                    r = [hop(ph, 1, -s, None, r, tag + ("r", s))]
                    l = [hop(ph, -1, s, None, l, tag + ("l", s))]
                    out += r + l
                out.append(hop(ph, 1, -3, 0, r, tag + ("r", 3)))
                out.append(hop(ph, -1, 3, 1, l, tag + ("l", 3)))
            elif ph == 2:
                r = hop(ph, 1, 0, 0, deps, tag + ("r", 0))
                l = hop(ph, -1, 0, 1, deps, tag + ("l", 0))
                out += [r, l, hop(ph, 1, 0, 1, deps, tag + ("r", 1)), hop(ph, -1, 0, 0, deps, tag + ("l", 1))]
                out += [hop(ph, 1, -1, 0, [r], tag + ("r", 2)), hop(ph, -1, 1, 1, [l], tag + ("l", 2))]
            else:
                r = hop(ph, 1, 0, None, deps, tag + ("r", 0))
                l = hop(ph, -1, 0, None, deps, tag + ("l", 0))
                out += [r, l, hop(ph, 1, -1, 0, [r], tag + ("r", 1)), hop(ph, -1, 1, 1, [l], tag + ("l", 1))]
            return out

        first = [direct(0, [], (t, kind, 0, "d"))]
        second = [direct(1, first, (t, kind, 1, "d"))] if 1 in DIRECT[kind] else ring(1, first)

        def hand_own():
            land(second)
            share(t, kind, region(2, me[dims[2]]))

        add((t, kind, 2, "own"), second, hand_own, rank=t * 10 + 4, loads={("core", 1): 16.0 * width})
        third = ring(2, second)
        return [(t, kind, 2, "own")] + [key + ("share",) for key in third]

    def share_wait(t):
        spans = ((MA, TILES[t][0]), (MB, (TILES[t][1][0], TILES[t][1][1] + TILES[t][2][1])))
        for n, (buf, span) in enumerate(spans):
            if span[1] == 0:
                continue
            copy = pltpu.make_async_remote_copy(
                src_ref=buf.at[core, pl.ds(*span)], dst_ref=buf.at[1 - core, pl.ds(*span)],
                send_sem=s_p.at[t, n], recv_sem=r_p.at[t, n], device_id=partner, device_id_type=MESH,
            )
            copy.wait_send()
            copy.wait_recv()

    def absorb(t, gs):
        for g in gs:
            gx, gy = g // 2, g % 2
            o = None
            for h in range(2):
                tiles = []
                for kind in range(3):
                    for u in range(TILES[t][kind][0], sum(TILES[t][kind])):
                        if kind == 0:
                            rows = [MA[h, u, z, gx, gy * 2 + j] for j in range(2) for z in range(8)]
                            tiles.append(jnp.concatenate(rows, axis=0))
                        else:
                            tiles.append(MB[h, u, gx, gy * 2 : gy * 2 + 2].reshape(256, 128))
                part_o = jnp.dot(jnp.concatenate(tiles, axis=1), X[h * 512 : (h + 1) * 512], preferred_element_type=F32)
                o = part_o if o is None else o + part_o
            o = o.reshape(16, 16, 256)
            re = o[:, :8, :128] - o[:, 8:, 128:]
            im = o[:, :8, 128:] + o[:, 8:, :128]
            Y[g * 128 : (g + 1) * 128, :128] = re.reshape(128, 128).astype(BF)
            Y[g * 128 : (g + 1) * 128, 128:] = im.reshape(128, 128).astype(BF)

    def put_next(k, p, block):
        S[pl.ds(p * 1024 + k, 128, stride=8), :] = block

    def enter():
        pl.semaphore_wait(barrier, 19)

    def to_plane():
        tell(plane, line_y)
        tell(square, cuts)

    def prepare_in():
        get_stem.wait()
        Y[:, :128] = stem[0]
        Y[:, 128:] = stem[1]

    def to_cube():
        pl.semaphore_wait(plane, 3)
        tell(cube, line_x)

    def all_in():
        pl.semaphore_wait(cube, 3)

    def prepare_out():
        snd1[...] = S[...].reshape(128, 16, 128).astype(BF)
        rcv1[m] = snd1[m]

    def start(t):
        if t == 0:
            exchange_wait(snd1, rcv1, 0)
            got = rcv1[...].astype(F32)
            X[:, :128] = got[:, :8, :].reshape(1024, 128).astype(BF)
            X[:, 128:] = got[:, 8:, :].reshape(1024, 128).astype(BF)
        else:
            X[:, :128] = S[:1024].astype(BF)
            X[:, 128:] = S[1024:].astype(BF)
        share_wait(t)

    pairs = ((0, 1), (2, 3), (4, 5), (6, 7))
    enter()
    shares = {}
    for t in range(3):
        shares[t] = []
        for kind in range(3):
            if TILES[t][kind][1] > 0:
                shares[t] += gather_item(t, kind)
    add("plane", [], to_plane, rank=1, start=0.5)
    add("in", [], prepare_in, rank=2, cost=0.3, start=0.6)
    last = ["in"]
    for n, ks in enumerate(pairs):
        add(("p", 0, n), last, functools.partial(permute, 0, put_send, ks), rank=2, cost=0.7)
        last = [("p", 0, n)]
    add("out", last, prepare_out, rank=2, cost=0.4)
    add("cube", ["plane"], to_cube, rank=2, start=3.5)
    add("all", ["cube"], all_in, rank=3, start=6.0)
    last = ["all", "out"]
    for n in range(8):
        lo, hi = max(1, n * 16), (n + 1) * 16
        add(("x", n), last, functools.partial(exchange, snd1, rcv1, 0, lo, hi), cost=0.6, rank=3,
            loads={(d, w): {"x": 40, "y": 64, "z": 80}[d] for d in "xyz" for w in (1, -1)}, start=6.0 + 0.8 * n)
    for n in range(4):
        add(("t", 1, n), [], functools.partial(make_pt, 1, pairs[n]), rank=50, cost=0.3, start=7.0)
        add(("t", 2, n), [], functools.partial(make_pt, 2, pairs[n]), rank=51, cost=0.3, start=7.0)
        add(("t", 3, n), [], functools.partial(make_rt, pairs[n]), rank=52, cost=0.4, start=7.0)
    ready = [("x", n) for n in range(8)]
    for t in range(3):
        add(("s", t), shares[t] + ready, functools.partial(start, t), cost=1.0, rank=30, start=0.0)
        last = [("s", t)]
        for n, gs in enumerate(pairs):
            add(("m", t, n), last, functools.partial(absorb, t, gs), cost=0.5, rank=30)
            last = [("m", t, n)]
        if t < 2:
            for n, ks in enumerate(pairs):
                add(("p", t + 1, n), last + [("t", t + 1, n)], functools.partial(permute, t + 1, put_next, ks), cost=0.5, rank=30)
                last = [("p", t + 1, n)]
        ready = last
    ordered = plan(tasks)
    for task in ordered:
        fns[task["key"]]()

    for p in range(2):
        for j in range(8):
            block = Y[j * 128 : (j + 1) * 128, p * 128 : (p + 1) * 128].astype(F32).T
            S[pl.ds(p * 8 + j, 128, stride=16), :] = block
            Y3T[p * 128 : (p + 1) * 128, j * 128 : (j + 1) * 128] = block.astype(BF)
    snd2[...] = S[...].reshape(128, 16, 128).astype(BF)
    exchange(snd2, rcv2, 1, 1, 64)
    rcv2[m] = snd2[m]

    place = lax.broadcasted_iota(jnp.int32, (128, 256), 0)
    for q in range(8):
        cols = cb[:, q * 256 : (q + 1) * 256]
        got = jnp.dot(Y3T[...], RT[q], preferred_element_type=F32)
        here = (place == cols // 128) & (cols % 128 == m)
        for p in range(2):
            val = jnp.sum(jnp.where(here, got[p * 128 : (p + 1) * 128], 0.0), axis=0, keepdims=True)
            a0[q * 2, p : p + 1, :] = val[:, :128]
            a0[q * 2 + 1, p : p + 1, :] = val[:, 128:]

    def spread(src_of, buf, peers, n):
        copies = []
        for k, peer in enumerate(peers):
            copy = pltpu.make_async_remote_copy(
                src_ref=src_of(k), dst_ref=buf.at[k + 1], send_sem=s_am.at[n, k], recv_sem=r_am.at[n, k],
                device_id=peer, device_id_type=MESH,
            )
            copy.start()
            copies.append(copy)
        return copies

    def collect(buf, copies, mine):
        total = mine
        for copy in copies:
            copy.wait()
        for k in range(len(copies)):
            total = total + buf[k + 1]
        return total

    pl.semaphore_wait(square, 3)
    face = [((c + i) % 4, (me["x"] + j) % 4) for i in range(4) for j in range(4) if i + j > 0]
    sheet = [((me["y"] + i) % 4, (me["z"] + j) % 8) for i in range(4) for j in range(8) if i + j > 0]
    one = spread(lambda k: a0.at[face[k][0] * 4 + face[k][1]], a1, [(i, mode_of(j, me["y"], me["z"])) for i, j in face], 0)
    exchange(snd2, rcv2, 1, 64, 128)
    a2[...] = collect(a1, one, a0[c * 4 + me["x"]])
    two = spread(lambda k: a2, a3, [(c, mode_of(me["x"], i, j)) for i, j in sheet], 1)
    for copy in sent:
        copy.wait_send()
    amp[...] = collect(a3, two, a2[...])

    exchange_wait(snd2, rcv2, 1)
    S[...] = rcv2[...].astype(F32).reshape(2048, 128)
    for p in range(2):
        for j in range(8):
            block = S[pl.ds(p * 8 + j, 128, stride=16), :]
            out[p, j * 128 : (j + 1) * 128, :] = block.T.astype(BF)


def body(stem, branches, order, swap_order, row_bits, column_bits):
    vmem = pl.BlockSpec(memory_space=pltpu.VMEM)
    br = branches.transpose(0, 1, 3, 2).reshape(3, 16, 1024)
    idx = swap_order.reshape(3, 128, 8)
    dma = pltpu.SemaphoreType.DMA
    field, amps = pl.pallas_call(
        kernel,
        out_shape=(jax.ShapeDtypeStruct((2, 1024, 128), BF), jax.ShapeDtypeStruct((2, 128), F32)),
        in_specs=[pl.BlockSpec(memory_space=pltpu.SMEM)] + [pl.BlockSpec(memory_space=pltpu.HBM)] * 2 + [vmem] * 3,
        out_specs=(vmem, vmem),
        scratch_shapes=[
            pltpu.VMEM((2, 1024, 128), BF),
            pltpu.VMEM((3, 16, 1024), BF),
            pltpu.VMEM((2, 3, 8, 4, 4, 16, 128), BF),
            pltpu.VMEM((2, 9, 4, 4, 8, 16, 128), BF),
            pltpu.VMEM((2, 1024, 1024), BF),
            pltpu.VMEM((8, 1024, 256), BF),
            pltpu.VMEM((1024, 256), BF),
            pltpu.VMEM((1024, 256), BF),
            pltpu.VMEM((2048, 128), F32),
            pltpu.VMEM((256, 1024), BF),
            pltpu.VMEM((128, 16, 128), BF),
            pltpu.VMEM((128, 16, 128), BF),
            pltpu.VMEM((128, 16, 128), BF),
            pltpu.VMEM((128, 16, 128), BF),
            pltpu.VMEM((16, 2, 128), F32),
            pltpu.VMEM((16, 2, 128), F32),
            pltpu.VMEM((2, 128), F32),
            pltpu.VMEM((32, 2, 128), F32),
            dma((2,)), dma((2,)),
            dma((9, 12)), dma((9, 12)),
            dma((3, 2)), dma((3, 2)),
            dma((2, 31)), dma((2, 31)),
            dma((2,)),
            pltpu.SemaphoreType.REGULAR, pltpu.SemaphoreType.REGULAR, pltpu.SemaphoreType.REGULAR,
        ],
        compiler_params=pltpu.CompilerParams(collective_id=0, has_side_effects=True, vmem_limit_bytes=63_000_000),
    )(order, stem[0], br, idx, row_bits.reshape(1, 2048), column_bits.reshape(1, 2048))
    m = lax.axis_index("mode")
    amps = lax.dynamic_slice_in_dim(amps, (m % 32) * 4, 4, 1)
    return field[None], amps


def solution(mesh):
    placed = (P("cuts", None, None, "mode"), P(None, None, None, "mode"), P(), P(), P(), P())
    return jax.shard_map(
        body,
        mesh=mesh,
        in_specs=placed,
        out_specs=(P("cuts", None, None, "mode"), P(None, ("cuts", "mode"))),
        check_vma=False,
    )
```

time: 99.8 us -> 92.7 us (0.929); the launches traced: 99.5 us -> 91.2 us
  Pallas kernels: 94.7 us -> 85.9 us
    pallas_call x1, Pallas kernels: 94.7 us -> 85.9 us  [body(): pl.pallas_call(kernel, out_shape=(jax.ShapeDtypeStruct((2, 1024, 128), BF...]
    unnamed x13 -> x5, local copies, waits for them, and re-layouts: 3.28 us -> 3.19 us
where the time goes in v3:
time: 92.7 us; the launch traced here: 91.2 us
  Pallas kernels  85.9 us (93%)
  local copies, waits for them, and re-layouts  4.64 us (5%)
    pallas_call x1, Pallas kernels, body(): pl.pallas_call(kernel, out_shape=(jax.ShapeDtypeStruct((2, 1024, 128), BF...  85.9 us
    unnamed x5, local copies, waits for them, and re-layouts  3.19 us

profile of v3, /device:TPU:6, one launch (start us, length us, event | category | flops | bytes accessed | tf_op | source)
XLA Modules:
  0.0 91.2 jit_solution(5473617511434115109)
XLA Ops:
  0.6 0.0 copy-start
  0.7 0.7 copy-done
  1.3 0.8 reshape.17.idx
  2.2 85.9 %shard_map.77 = (bf16[2,1024,128]{2,1,0:T(8,128)(2,1)}, f32[2,128]{1,0:T(2,128)}) custom-call(s32[3]{0:T(128)} %order.1, bf16[2,1024,128]{2,1,0:T(8,128)(2,1)} %bitcast.7, bf16[3,16,1024]{2,1,0:T(8,128)(2,1)} %bitcast.9, s32[3,128,8]{2,1,0:T(8,128)} %reshape.17.idx, s32[1,2048]{1,0:T(1,128)} %bitcast.10, s32[1,2048]{1,0:T(1,128)} %bitcast.11), custom_call_target="tpu_custom_call" | custom-call | tf_op jit(solution)/shard_map/pallas_call | solution.py:450
  88.1 0.0 copy-start.1
  88.1 0.6 copy-done.1
  88.7 0.6 constant_dynamic-slice_fusion
  89.3 1.9 %copy.9 = bf16[1,2,1024,128]{3,2,1,0:T(8,128)(2,1)} copy(bf16[1,2,1024,128]{3,2,1,0:T(8,128)(2,1)} %bitcast.8) | data formatting | bytes 1048576
Async XLA Ops:
  0.6 0.7 copy-start
  88.1 0.6 copy-start.1

commit v4 on v3

--- a/solution.py
+++ b/solution.py
@@ -478,7 +478,7 @@
             dma((2,)),
             pltpu.SemaphoreType.REGULAR, pltpu.SemaphoreType.REGULAR, pltpu.SemaphoreType.REGULAR,
         ],
-        compiler_params=pltpu.CompilerParams(collective_id=0, has_side_effects=True, vmem_limit_bytes=63_000_000),
+        compiler_params=pltpu.CompilerParams(collective_id=0, has_side_effects=True, vmem_limit_bytes=48_000_000),
     )(order, stem[0], br, idx, row_bits.reshape(1, 2048), column_bits.reshape(1, 2048))
     m = lax.axis_index("mode")
     amps = lax.dynamic_slice_in_dim(amps, (m % 32) * 4, 4, 1)

time: 92.7 us -> 91 us (0.982)
  Pallas kernels: 85.9 us -> 84.9 us
    pallas_call x1, Pallas kernels: 85.9 us -> 84.9 us  [body(): pl.pallas_call(kernel, out_shape=(jax.ShapeDtypeStruct((2, 1024, 128), BF...]
    unnamed x5 -> x13, local copies, waits for them, and re-layouts: 3.19 us -> 3.28 us
where the time goes in v4:
time: 91 us; the launch traced here: 89.6 us
  Pallas kernels  84.9 us (93%)
  local copies, waits for them, and re-layouts  4.05 us (4%)
    pallas_call x1, Pallas kernels, body(): pl.pallas_call(kernel, out_shape=(jax.ShapeDtypeStruct((2, 1024, 128), BF...  84.9 us
    unnamed x13, local copies, waits for them, and re-layouts  3.28 us

profile of v4, /device:TPU:6, one launch (start us, length us, event | category | flops | bytes accessed | tf_op | source)
XLA Modules:
  0.0 89.6 jit_solution(7305872046455976730)
XLA Ops:
  0.6 0.0 copy-start.5
  0.7 0.7 copy-done.5
  1.4 0.0 copy-start.1
  1.4 0.0 copy-start.2
  1.4 0.0 copy-start.3
  1.4 0.1 reshape.17.idx
  1.5 0.0 copy-start.4
  1.5 0.7 copy-done.1
  2.2 0.0 copy-done.2
  2.2 0.0 copy-done.3
  2.2 0.0 copy-done.4
  2.3 0.0 copy-start
  2.3 1.0 %copy-done = bf16[1,2,1024,128]{3,2,1,0:T(8,128)(2,1)S(1)} copy-done((bf16[1,2,1024,128]{3,2,1,0:T(8,128)(2,1)S(1)}, bf16[1,2,1024,128]{3,2,1,0:T(8,128)(2,1)}, u32[]{:S(2)}) %copy-start) | copy-done | bytes 524312
  3.3 84.9 %shard_map.77 = (bf16[2,1024,128]{2,1,0:T(8,128)(2,1)S(1)}, f32[2,128]{1,0:T(2,128)S(1)}) custom-call(s32[3]{0:T(128)S(1)} %copy-done.4, bf16[2,1024,128]{2,1,0:T(8,128)(2,1)S(1)} %bitcast.7, bf16[3,16,1024]{2,1,0:T(8,128)(2,1)S(1)} %bitcast.9, s32[3,128,8]{2,1,0:T(8,128)S(1)} %reshape.17.idx, s32[1,2048]{1,0:T(1,128)S(1)} %bitcast.10, s32[1,2048]{1,0:T(1,128)S(1)} %bitcast.11), custom_call_target="tpu_custom_call" | custom-call | tf_op jit(solution)/shard_map/pallas_call | solution.py:450
  88.2 0.6 constant_dynamic-slice_fusion
  88.8 0.8 copy.9
Async XLA Ops:
  0.6 0.7 copy-start.5
  1.4 0.9 copy-start.1
  1.4 0.9 copy-start.2
  1.4 0.9 copy-start.3
  1.5 0.8 copy-start.4
  2.3 1.0 %copy-start = (bf16[1,2,1024,128]{3,2,1,0:T(8,128)(2,1)S(1)}, bf16[1,2,1024,128]{3,2,1,0:T(8,128)(2,1)}, u32[]{:S(2)}) copy-start(bf16[1,2,1024,128]{3,2,1,0:T(8,128)(2,1)} %param.6) | copy-start | bytes 1572868
